TPU v7x, 256 devices: a whole 4x4x8 slice. The times are simulated.
256 devices in a mesh: cell: 32 (over z_hi, x, core), mode: 8 (over z_lo, y).
Axes of the slice: x: 4, y: 4, z: 8 (z_hi: 4, z_lo: 2; z = z_hi * 2 + z_lo), core: 2. Of those that a mesh axis runs over, the one named last changes fastest.
Arguments:
- pod_modes: bfloat16 [3, 512, 4, 64, 128], P(None, 'mode', None, 'cell'), may hold values from -6 to 6
- slab_map: int32 [4, 64, 128], P(None, 'cell'), may hold values from 0 to 7
- slab_volume: float32 [8], replicated, may hold values from 0.25 to 4
- advect_index: int32 [8], replicated, may hold values from 0 to 511, as said below
- pair_adv: int32 [2048], replicated, may hold values from 0 to 7
- pair_mode: int32 [2048], replicated, may hold values from 0 to 511
- pair_amp: float32 [2048, 1024], replicated, may hold values from -0.2 to 0.2
Outputs:
- convective: float32 [512, 8, 512], P(('mode', 'cell'))
- response: float32 [512, 1024], P(('mode', 'cell'))
Inputs may be any that keep to these rules, and one draw needn't show every extreme that they name: `advect_index`: 8 distinct mode indices.
All inputs are finite; a program needn't handle non-finite values.
Results may differ from a plain program's by a relative error of at most 0.0043.
Values may be sent and summed in bfloat16 or wider, within the bound.
A program may use at most 128 MiB of HBM per device.

v0:
```python
import jax
import jax.numpy as jnp
from jax import lax
from jax.sharding import PartitionSpec as P


def split_up(x, dim, size):
    lengths = x.shape
    blocks = x.reshape(*lengths[:dim], size, lengths[dim] // size, *lengths[dim + 1 :])
    return jnp.moveaxis(blocks, dim, 0)


def sum_at_owner(x, axis, dim):
    blocks = split_up(x, dim, lax.axis_size(axis))
    arrived = lax.all_to_all(blocks, axis, split_axis=0, concat_axis=0, tiled=True)
    return arrived.sum(axis=0)


def padded(x, sides, width):
    for axis, dim in sides:
        size, length = (lax.axis_size(axis), x.shape[dim])
        up = [(i, (i + 1) % size) for i in range(size - 1)]
        down = [(j, i) for i, j in up]
        last = lax.slice_in_dim(x, length - width, length, axis=dim)
        first = lax.slice_in_dim(x, 0, width, axis=dim)
        before = lax.ppermute(last, axis, up)
        after = lax.ppermute(first, axis, down)
        x = jnp.concatenate([before, x, after], axis=dim)
    return x


def from_everyone(x, axis):
    copies = jnp.broadcast_to(x, (lax.axis_size(axis), *x.shape))
    return lax.all_to_all(copies, axis, split_axis=0, concat_axis=0, tiled=True)


def of_everyone(x, axis):
    everything = from_everyone(x, axis)
    return jnp.sum(everything.astype(jnp.float32), axis=0)


def gradients(haloed):
    interior = haloed[:, :, :, 1:-1].astype(jnp.float32)
    along_x = 0.5 * (jnp.roll(interior, -1, axis=2) - jnp.roll(interior, 1, axis=2))
    along_y = 0.5 * (
        haloed[:, :, :, 2:].astype(jnp.float32) - haloed[:, :, :, :-2].astype(jnp.float32)
    )
    along_z = 0.5 * (jnp.roll(interior, -1, axis=4) - jnp.roll(interior, 1, axis=4))
    return jnp.stack([along_x, along_y, along_z]).astype(jnp.bfloat16)


def contract(left_factor, grads):
    return jnp.einsum("ijdcxyz,dckxyz->ijk", left_factor, grads, preferred_element_type=jnp.float32)


def owner_rows(partial_value):
    return sum_at_owner(partial_value, "cell", 0)


def shards(pod_modes, slab_map, slab_volume, advect_index, pair_adv, pair_mode, pair_amp):
    mode_block = pod_modes.shape[1]
    planes = pod_modes.shape[2]
    rows_y = pod_modes.shape[3]
    cols_z = pod_modes.shape[4]
    mode_devs = lax.axis_size("mode")
    cell_devs = lax.axis_size("cell")
    mode_count = mode_block * mode_devs
    advect_count = advect_index.shape[0]
    scale_factor = float(planes * rows_y * cell_devs * cols_z) ** (-0.5)
    haloed = padded(pod_modes, (("cell", 3),), 1)
    first_mode = lax.axis_index("mode") * mode_block
    slots = lax.broadcasted_iota(jnp.int32, (advect_count, mode_block), 1)
    owned = (advect_index[:, None] == first_mode + slots).astype(jnp.bfloat16)
    picked = jnp.einsum("jm,cmxyz->cjxyz", owned, pod_modes, preferred_element_type=jnp.float32)
    chosen = of_everyone(picked.astype(jnp.bfloat16), "mode").astype(jnp.float32)
    levels = slab_volume.shape[0]
    level_ids = lax.broadcasted_iota(jnp.int32, (levels, planes, rows_y, cols_z), 0)
    volume = jnp.sum(
        jnp.where(slab_map[None] == level_ids, slab_volume[:, None, None, None], 0.0), axis=0
    )
    weighted = chosen * volume[None, None]
    left_factor = (
        jnp.transpose(pod_modes, (1, 0, 2, 3, 4))[:, None, None, :].astype(jnp.float32)
        * jnp.transpose(weighted, (1, 0, 2, 3, 4))[None, :, :, None]
    ).astype(jnp.bfloat16)
    local_grads = gradients(haloed)
    block_part = contract(left_factor, lax.all_gather(local_grads, "mode", axis=2, tiled=True))
    owned_rows = owner_rows(block_part)
    tensor = owned_rows * scale_factor
    flat_rows = tensor.reshape(tensor.shape[0], advect_count * mode_count)
    pair_slot = pair_adv * mode_count + pair_mode
    columns = jnp.take(flat_rows, pair_slot, axis=1)
    response = jnp.dot(
        columns, pair_amp, precision=lax.Precision.HIGHEST, preferred_element_type=jnp.float32
    )
    return (tensor, response)


def solution(mesh):
    in_specs = (P(None, "mode", None, "cell", None), P(None, "cell", None), P(), P(), P(), P(), P())
    out_specs = (P(("mode", "cell"), None, None), P(("mode", "cell"), None))
    return jax.shard_map(shards, mesh=mesh, in_specs=in_specs, out_specs=out_specs, check_vma=False)
```

profile of v0, /device:TPU:32, one launch (start us, length us, event | category | flops | bytes accessed | tf_op | source)
XLA Modules:
  0.0 200.7 jit_solution(4320587217358106295)
XLA Ops:
  7.2 0.0 all-gather.2.cloned.1.call-start
  7.2 1.2 convert_bitcast_fusion
  8.4 0.8 fusion.23
  9.2 1.3 collective-permute-start
  10.5 3.7 %collective-permute-start.1 = (bf16[3,64,4,1,128]{4,1,3,2,0:T(8,128)(2,1)}, bf16[3,64,4,1,128]{4,1,3,2,0:T(8,128)(2,1)}, u32[]{:S(2)}, u32[]{:S(2)}) collective-permute-start(bf16[3,64,4,1,128]{4,1,3,2,0:T(8,128)(2,1)} %get-tuple-element.14), channel_id=1, source_target_pairs={{0,8},{8,16},{16,24},{24,32},{32,40},{40,48},{48,56},{56,64},{64,7... | collective-permute-start | bytes 589832 | tf_op jit(solution)/shard_map/ppermute | solution.py:26
  14.2 0.3 fusion.22
  14.5 1.2 slice_bitcast_fusion
  15.7 1.2 slice_bitcast_fusion.2
  16.9 0.8 slice_bitcast_fusion.4
  17.7 0.0 copy-start.3
  17.7 0.3 copy.49
  18.0 0.3 copy.50
  18.3 0.3 copy.51
  18.6 0.3 copy.52
  19.0 0.0 copy-start.4
  19.0 0.0 copy-start.5
  19.0 2.2 %fusion.9 = (bf16[1,3,64,4,2,128]{5,2,4,3,0,1:T(8,128)(2,1)S(1)}, bf16[1,3,64,4,2,128]{5,2,4,3,0,1:T(8,128)(2,1)S(1)}) fusion(f32[1,3,64,1,2,128]{5,2,4,3,1,0:T(8,128)} %get-tuple-element.3, f32[1,3,64,3,2,128]{5,2,4,3,1,0:T(8,128)} %get-tuple-element.5, f32[1,3,64,3,2,128]{5,2,4,3,0,1:T(8,128)} %get-tuple-element.4, ...), kind=kLoop, calls=%fused_computation.16 | loop fusion | flops 1966080 | bytes 3932160 | tf_op jit(solution)/shard_map/convert.1
  21.2 0.0 collective-permute-done
  21.2 0.0 collective-permute-done.1
  21.3 1.2 fusion.15
  22.4 1.2 pad_maximum_fusion
  23.6 0.0 all-gather.2.cloned.1.call-update
  23.6 0.0 copy-done.4
  23.6 1.2 fusion.4
  24.9 0.8 broadcast_in_dim.33
  25.7 5.9 %all-to-all-start = ((bf16[8,3,8,4,2,128]{5,2,4,3,1,0:T(8,128)(2,1)}), bf16[8,3,8,4,2,128]{5,2,4,3,1,0:T(8,128)(2,1)S(1)}, u32[]{:S(2)}, u32[]{:S(2)}) async-start(bf16[8,3,8,4,2,128]{5,2,4,3,1,0:T(8,128)(2,1)} %broadcast_in_dim.33), calls=%async_computation | async-start | bytes 786432 | tf_op jit(solution)/shard_map/all_to_all | solution.py:34
  31.6 0.6 copy.40
  32.2 0.0 copy-done.3
  32.3 0.0 copy-done.5
  32.3 0.1 select_reduce_fusion
  32.4 7.1 %all-to-all-done = bf16[8,3,8,4,2,128]{5,2,4,3,1,0:T(8,128)(2,1)S(1)} async-done(((bf16[8,3,8,4,2,128]{5,2,4,3,1,0:T(8,128)(2,1)}), bf16[8,3,8,4,2,128]{5,2,4,3,1,0:T(8,128)(2,1)S(1)}, u32[]{:S(2)}, u32[]{:S(2)}) %all-to-all-start) | async-done | bytes 393248 | tf_op jit(solution)/shard_map/all_to_all | solution.py:34
  39.5 0.1 convert_reduce_fusion
  39.5 0.0 copy-start.1
  39.6 0.0 copy-start.2
  39.6 92.9 %all-gather.2.cloned.1.call-done = bf16[3,3,512,4,2,128]{5,2,4,3,0,1:T(8,128)(2,1)} async-done(((bf16[3,3,64,4,2,128]{5,2,4,3,0,1:T(8,128)(2,1)}), bf16[3,3,512,4,2,128]{5,2,4,3,0,1:T(8,128)(2,1)}) %all-gather.2.cloned.1.call-update) | async-done | bytes 9437200 | tf_op jit(solution)/shard_map/all_gather | solution.py:87
  132.4 8.4 %fusion = f32[64,8,512,1,1,1,1]{2,1,6,0,5,4,3:T(8,128)} fusion(bf16[3,3,512,4,2,128]{5,2,4,3,0,1:T(8,128)(2,1)} %all-gather.2.cloned.1.call-done, f32[8,3,4,2,128]{4,0,3,2,1:T(8,128)S(1)} %multiply_bitcast_fusion, f32[64,3,4,2,128]{4,3,0,2,1:T(2,128)S(1)} %copy.40), kind=kOutput, calls=%fused_computation.2 | convolution fusion | flops 4841275392 | bytes 11370496 | tf_op jit(solution)/shard_map/ijdcxyz,dckxyz->ijk/dot_general | solution.py:53
  140.8 9.8 %all-to-all-start.1 = ((f32[32,2,8,512]{3,2,1,0:T(8,128)}), f32[32,2,8,512]{3,2,1,0:T(8,128)S(1)}, u32[]{:S(2)}, u32[]{:S(2)}) async-start(f32[32,2,8,512]{3,2,1,0:T(8,128)} %bitcast.22), calls=%async_computation.1 | async-start | bytes 2097152 | tf_op jit(solution)/shard_map/all_to_all | solution.py:15
  150.7 0.0 copy-done.1
  150.7 0.0 copy-done.2
  150.7 29.8 %all-to-all-done.1 = f32[32,2,8,512]{3,2,1,0:T(8,128)S(1)} async-done(((f32[32,2,8,512]{3,2,1,0:T(8,128)}), f32[32,2,8,512]{3,2,1,0:T(8,128)S(1)}, u32[]{:S(2)}, u32[]{:S(2)}) %all-to-all-start.1) | async-done | bytes 1048608 | tf_op jit(solution)/shard_map/all_to_all | solution.py:15
  180.5 0.1 reduce_sum.29
  180.6 0.0 copy-start
  180.6 0.6 copy.54
  181.3 5.5 %gather_fusion = f32[2048,2]{1,0:T(8,128)S(1)} fusion(f32[2,4096]{0,1:T(8,128)S(1)} %bitcast.57, s32[2048]{0:T(1024)S(1)} %broadcast_clamp_fusion), kind=kCustom, calls=%fused_computation | custom fusion | bytes 40960 | tf_op jit(solution)/shard_map/jit(_take)/gather | solution.py:92
  186.7 7.1 %fusion.5 = f32[2,1024]{1,0:T(2,128)} fusion(f32[2048,1024]{1,0:T(8,128)} %param.13, f32[2048,2]{1,0:T(8,128)S(1)} %gather_fusion, pred[2048]{0:T(1024)(128)(4,1)S(1)} %compare_and_fusion), kind=kOutput, calls=%fused_computation.9 | convolution fusion | flops 50335744 | bytes 8415232 | tf_op jit(solution)/shard_map/dot_general | solution.py:93
  193.9 0.0 copy-done
  (5 shorter events, 0.0 us)
Async XLA Ops:
  7.2 125.3 %all-gather.2.cloned.1.call-start = ((), (), s32[]{:S(2)}) async-start(), calls=%async_computation.2 | async-start | bytes 10616832 | tf_op jit(solution)/shard_map/all_gather | solution.py:87
  9.2 12.0 %collective-permute-start = (bf16[3,64,4,1,128]{4,1,3,2,0:T(8,128)(2,1)}, bf16[3,64,4,1,128]{4,1,3,2,0:T(8,128)(2,1)}, u32[]{:S(2)}, u32[]{:S(2)}) collective-permute-start(bf16[3,64,4,1,128]{4,1,3,2,0:T(8,128)(2,1)} %get-tuple-element.13), channel_id=1, source_target_pairs={{8,0},{16,8},{24,16},{32,24},{40,32},{48,40},{56,48},{64,56},{72,6... | collective-permute-start | bytes 589832 | tf_op jit(solution)/shard_map/ppermute | solution.py:27
  10.5 10.7 %collective-permute-start.1 = (bf16[3,64,4,1,128]{4,1,3,2,0:T(8,128)(2,1)}, bf16[3,64,4,1,128]{4,1,3,2,0:T(8,128)(2,1)}, u32[]{:S(2)}, u32[]{:S(2)}) collective-permute-start(bf16[3,64,4,1,128]{4,1,3,2,0:T(8,128)(2,1)} %get-tuple-element.14), channel_id=1, source_target_pairs={{0,8},{8,16},{16,24},{24,32},{32,40},{40,48},{48,56},{56,64},{64,7... | collective-permute-start | bytes 589832 | tf_op jit(solution)/shard_map/ppermute | solution.py:26
  17.7 14.6 %copy-start.3 = (s32[4,2,128]{2,1,0:T(2,128)S(1)}, s32[4,2,128]{2,1,0:T(2,128)}, u32[]{:S(2)}) copy-start(s32[4,2,128]{2,1,0:T(2,128)} %param.8) | copy-start | bytes 12292
  19.0 4.7 %copy-start.4 = (s32[8]{0:T(128)S(1)}, s32[8]{0:T(128)}, u32[]{:S(2)}) copy-start(s32[8]{0:T(128)} %param.10) | copy-start | bytes 100
  19.0 13.3 %copy-start.5 = (f32[8]{0:T(128)S(1)}, f32[8]{0:T(128)}, u32[]{:S(2)}) copy-start(f32[8]{0:T(128)} %param.9) | copy-start | bytes 100
  25.7 13.8 %all-to-all-start = ((bf16[8,3,8,4,2,128]{5,2,4,3,1,0:T(8,128)(2,1)}), bf16[8,3,8,4,2,128]{5,2,4,3,1,0:T(8,128)(2,1)S(1)}, u32[]{:S(2)}, u32[]{:S(2)}) async-start(bf16[8,3,8,4,2,128]{5,2,4,3,1,0:T(8,128)(2,1)} %broadcast_in_dim.33), calls=%async_computation | async-start | bytes 786432 | tf_op jit(solution)/shard_map/all_to_all | solution.py:34
  39.5 111.1 %copy-start.1 = (s32[2048]{0:T(1024)S(1)}, s32[2048]{0:T(1024)}, u32[]{:S(2)}) copy-start(s32[2048]{0:T(1024)} %param.12) | copy-start | bytes 24580
  39.6 111.1 %copy-start.2 = (s32[2048]{0:T(1024)S(1)}, s32[2048]{0:T(1024)}, u32[]{:S(2)}) copy-start(s32[2048]{0:T(1024)} %param.11) | copy-start | bytes 24580
  140.8 39.7 %all-to-all-start.1 = ((f32[32,2,8,512]{3,2,1,0:T(8,128)}), f32[32,2,8,512]{3,2,1,0:T(8,128)S(1)}, u32[]{:S(2)}, u32[]{:S(2)}) async-start(f32[32,2,8,512]{3,2,1,0:T(8,128)} %bitcast.22), calls=%async_computation.1 | async-start | bytes 2097152 | tf_op jit(solution)/shard_map/all_to_all | solution.py:15
  180.6 13.3 %copy-start = (f32[2,8,512]{2,1,0:T(8,128)}, f32[2,8,512]{2,1,0:T(8,128)S(1)}, u32[]{:S(2)}) copy-start(f32[2,8,512]{2,1,0:T(8,128)S(1)} %broadcast_multiply_fusion) | copy-start | bytes 98308
Sparse Core Ops, SparseCore 0:
  23.7 108.6 all-gather.1
where the time goes:
time: 201 us
  waiting for transfers between devices  130 us (65%)
  starting transfers between devices  20.8 us (10%)
  matrix products  16.8 us (8%)
  between operations  14.2 us (7%)
  local copies, waits for them, and re-layouts  13.1 us (7%)
  other arithmetic  6.06 us (3%)
    all_gather x1, waiting for transfers between devices, shards(): lax.all_gather(local_grads, 'mode', axis=2, tiled=True)  92.9 us
    all_to_all x1, waiting for transfers between devices, sum_at_owner(): lax.all_to_all(blocks, axis, split_axis=0, concat_axis=0, tiled=True)  29.8 us
    all_to_all x1, starting transfers between devices, sum_at_owner(): lax.all_to_all(blocks, axis, split_axis=0, concat_axis=0, tiled=True)  9.82 us
    dot_general x1, matrix products, contract(): jnp.einsum('ijdcxyz,dckxyz->ijk', left_factor, grads, preferred_element_t...  8.4 us
    dot_general x1, matrix products, shards(): jnp.dot(columns, pair_amp, precision=lax.Precision.HIGHEST, preferred_ele...  7.14 us
    all_to_all x1, waiting for transfers between devices, from_everyone(): return lax.all_to_all(copies, axis, split_axis=0, concat_axis=0, tiled=True)  7.12 us
    all_to_all x1, starting transfers between devices, from_everyone(): return lax.all_to_all(copies, axis, split_axis=0, concat_axis=0, tiled=True)  5.93 us
    gather x1, local copies, waits for them, and re-layouts, shards(): columns = jnp.take(flat_rows, pair_slot, axis=1)  5.47 us
  transfers between devices with their start and end apart: 5, of which 3 were waited for; matrix products, arithmetic and copies ran while one was open for 5% of the time, Pallas kernels for 0%

commit v1 on v0

--- a/solution.py
+++ b/solution.py
@@ -1,7 +1,19 @@
+import functools
 import jax
 import jax.numpy as jnp
 from jax import lax
 from jax.sharding import PartitionSpec as P
+
+
+def copies_cover(inputs, axis_name, row_dim):
+    v1 = lax.axis_size(axis_name)
+    built = jnp.stack(v1 * [inputs], 0)
+    near = lax.all_to_all(built, axis_name, 0, 0)
+    all_values = jnp.concatenate(near, row_dim)
+    return all_values
+
+
+guide_sums_all_on = functools.partial(copies_cover, axis_name="mode", row_dim=2)
 
 
 def split_up(x, dim, size):
@@ -84,7 +96,7 @@
         * jnp.transpose(weighted, (1, 0, 2, 3, 4))[None, :, :, None]
     ).astype(jnp.bfloat16)
     local_grads = gradients(haloed)
-    block_part = contract(left_factor, lax.all_gather(local_grads, "mode", axis=2, tiled=True))
+    block_part = contract(left_factor, guide_sums_all_on(local_grads))
     owned_rows = owner_rows(block_part)
     tensor = owned_rows * scale_factor
     flat_rows = tensor.reshape(tensor.shape[0], advect_count * mode_count)

time: 201 us -> 225 us (1.12)
  local copies, waits for them, and re-layouts: 13.1 us -> 35.2 us
  between operations: 14.2 us -> 0.83 us
  starting transfers between devices: 20.8 us -> 27.2 us
  other arithmetic: 6.06 us -> 11.1 us
  waiting for transfers between devices: 130 us -> 133 us
    all_to_all x0 -> x1, waiting for transfers between devices: none -> 103 us  [copies_cover(): near = lax.all_to_all(built, axis_name, 0, 0)]
    all_gather x1 -> x0, waiting for transfers between devices: 92.9 us -> none  [shards(): lax.all_gather(local_grads, 'mode', axis=2, tiled=True)]
    reshape x0 -> x1, local copies, waits for them, and re-layouts: none -> 10.7 us  [copies_cover(): all_values = jnp.concatenate(near, row_dim)]
    all_to_all x1, waiting for transfers between devices: 7.12 us -> 0.01 us  [from_everyone(): return lax.all_to_all(copies, axis, split_axis=0, concat_axis=0, tiled=True)]
    another operation x0 -> x2, local copies, waits for them, and re-layouts: none -> 6.41 us  [the longest x1 6.11 us: copies_cover(): built = jnp.stack(v1 * [inputs], 0)]
    all_to_all x0 -> x1, starting transfers between devices: none -> 5.84 us  [copies_cover(): near = lax.all_to_all(built, axis_name, 0, 0)]
    another operation x2, other arithmetic: 2.33 us -> 4.96 us  [gradients(): return jnp.stack([along_x, along_y, along_z]).astype(jnp.bfloat16)]
  transfers between devices with their start and end apart: 5 -> 5, of which waited for: 3 -> 2; matrix products, arithmetic and copies ran while one was open for 5% -> 10% of each run, Pallas kernels for 0% -> 0%
where the time goes in v1:
time: 225 us; the launch traced here: 224 us
  waiting for transfers between devices  133 us (59%)
  local copies, waits for them, and re-layouts  35.2 us (16%)
  starting transfers between devices  27.2 us (12%)
  matrix products  16.8 us (7%)
  other arithmetic  11.1 us (5%)
    all_to_all x1, waiting for transfers between devices, copies_cover(): near = lax.all_to_all(built, axis_name, 0, 0)  103 us
    all_to_all x1, waiting for transfers between devices, sum_at_owner(): lax.all_to_all(blocks, axis, split_axis=0, concat_axis=0, tiled=True)  29.8 us
    reshape x1, local copies, waits for them, and re-layouts, copies_cover(): all_values = jnp.concatenate(near, row_dim)  10.7 us
    all_to_all x1, starting transfers between devices, sum_at_owner(): lax.all_to_all(blocks, axis, split_axis=0, concat_axis=0, tiled=True)  10.4 us
    dot_general x1, matrix products, contract(): jnp.einsum('ijdcxyz,dckxyz->ijk', left_factor, grads, preferred_element_t...  8.44 us
    dot_general x1, matrix products, shards(): jnp.dot(columns, pair_amp, precision=lax.Precision.HIGHEST, preferred_ele...  7.14 us
    another operation x1, local copies, waits for them, and re-layouts, copies_cover(): built = jnp.stack(v1 * [inputs], 0)  6.11 us
    all_to_all x1, starting transfers between devices, from_everyone(): return lax.all_to_all(copies, axis, split_axis=0, concat_axis=0, tiled=True)  5.93 us
  transfers between devices with their start and end apart: 5, of which 2 were waited for; matrix products, arithmetic and copies ran while one was open for 10% of the time, Pallas kernels for 0%

profile of v1, /device:TPU:32, one launch (start us, length us, event | category | flops | bytes accessed | tf_op | source)
XLA Modules:
  0.0 224.1 jit_solution(17770327876457495778)
XLA Ops:
  0.6 0.0 copy-start
  0.6 2.8 %fusion.20 = (bf16[3,64,4,1,128]{4,3,2,1,0:T(2,128)(2,1)}, bf16[3,64,4,1,128]{4,3,2,1,0:T(2,128)(2,1)}) fusion(bf16[3,64,4,2,128]{4,3,2,1,0:T(2,128)(2,1)} %param.7), kind=kLoop, calls=%fused_computation.44 | loop fusion | bytes 786432 | tf_op jit(solution)/shard_map/slice | solution.py:37
  3.4 1.3 collective-permute-start
  4.7 3.8 %collective-permute-start.1 = (bf16[3,64,4,1,128]{4,3,2,1,0:T(2,128)(2,1)}, bf16[3,64,4,1,128]{4,3,2,1,0:T(2,128)(2,1)}, u32[]{:S(2)}, u32[]{:S(2)}) collective-permute-start(bf16[3,64,4,1,128]{4,3,2,1,0:T(2,128)(2,1)} %get-tuple-element.9), channel_id=1, source_target_pairs={{0,8},{8,16},{16,24},{24,32},{32,40},{40,48},{48,56},{56,64},{64,7... | collective-permute-start | bytes 589832 | tf_op jit(solution)/shard_map/ppermute | solution.py:38
  8.5 1.2 fusion.4
  9.7 0.8 broadcast_in_dim.33
  10.6 5.9 %all-to-all-start = ((bf16[8,3,8,4,2,128]{5,2,4,3,1,0:T(8,128)(2,1)}), bf16[8,3,8,4,2,128]{5,2,4,3,1,0:T(8,128)(2,1)}, u32[]{:S(2)}, u32[]{:S(2)}) async-start(bf16[8,3,8,4,2,128]{5,2,4,3,1,0:T(8,128)(2,1)} %broadcast_in_dim.33), calls=%async_computation | async-start | bytes 786432 | tf_op jit(solution)/shard_map/all_to_all | solution.py:46
  16.5 1.3 mul.91
  17.8 2.0 slice_bitcast_fusion
  19.7 1.5 slice_bitcast_fusion.2
  21.2 0.9 slice_bitcast_fusion.4
  22.1 0.0 copy-done
  22.1 0.7 fusion.21
  22.8 0.8 copy.41
  23.6 0.9 copy.42
  24.5 0.8 copy.43
  25.3 0.9 copy.44
  26.2 3.6 %fusion.8 = (bf16[1,3,64,4,2,128]{5,4,3,2,1,0:T(2,128)(2,1)S(1)}, bf16[1,3,64,4,2,128]{5,4,3,2,1,0:T(2,128)(2,1)S(1)}) fusion(f32[1,3,64,1,2,128]{5,4,3,2,1,0:T(2,128)} %get-tuple-element.3, f32[1,3,64,3,2,128]{5,4,3,2,1,0:T(2,128)} %get-tuple-element.5, f32[1,3,64,3,2,128]{5,4,3,2,1,0:T(2,128)} %get-tuple-element.4, ...), kind=kLoop, calls=%fused_computation.15 | loop fusion | flops 1966080 | bytes 3932160 | tf_op jit(solution)/shard_map/convert.2
  29.8 0.0 collective-permute-done
  29.8 0.0 collective-permute-done.1
  29.8 2.9 %fusion.13 = bf16[1,3,64,4,2,128]{5,4,3,2,1,0:T(2,128)(2,1)S(1)} fusion(bf16[3,64,4,2,128]{4,3,2,1,0:T(2,128)(2,1)S(1)} %copy-done, bf16[3,64,4,1,128]{4,3,2,1,0:T(2,128)(2,1)} %collective-permute-done.1, bf16[3,64,4,1,128]{4,3,2,1,0:T(2,128)(2,1)} %collective-permute-done), kind=kLoop, calls=%fused_computation.25 | loop fusion | flops 2162688 | bytes 1179648 | tf_op jit(solution)/shard_map/stack | solution.py:61
  32.8 2.0 pad_maximum_fusion
  34.8 0.3 copy.45
  35.1 0.0 all-to-all-done
  35.1 6.1 %stack.8 = bf16[8,3,3,64,4,2,128]{6,3,5,4,1,2,0:T(8,128)(2,1)} broadcast(bf16[3,3,64,4,2,128]{5,2,4,3,0,1:T(8,128)(2,1)S(1)} %copy.45), dimensions={1,2,3,4,5,6} | broadcast | bytes 10616832 | tf_op jit(solution)/shard_map/stack | solution.py:10
  41.2 0.0 copy-start.4
  41.3 0.0 copy-start.5
  41.3 5.8 %all-to-all-start.1 = ((bf16[8,3,3,64,4,2,128]{6,3,5,4,1,2,0:T(8,128)(2,1)}), bf16[8,3,3,64,4,2,128]{6,3,5,4,1,2,0:T(8,128)(2,1)}, u32[]{:S(2)}, u32[]{:S(2)}) async-start(bf16[8,3,3,64,4,2,128]{6,3,5,4,1,2,0:T(8,128)(2,1)} %stack.8), calls=%async_computation.1 | async-start | bytes 18874368 | tf_op jit(solution)/shard_map/all_to_all | solution.py:11
  47.1 0.0 copy-done.4
  47.1 0.0 copy-done.5
  47.1 0.1 select_reduce_fusion
  47.2 1.1 convert_reduce_fusion
  48.3 103.1 %all-to-all-done.1 = bf16[8,3,3,64,4,2,128]{6,3,5,4,1,2,0:T(8,128)(2,1)} async-done(((bf16[8,3,3,64,4,2,128]{6,3,5,4,1,2,0:T(8,128)(2,1)}), bf16[8,3,3,64,4,2,128]{6,3,5,4,1,2,0:T(8,128)(2,1)}, u32[]{:S(2)}, u32[]{:S(2)}) %all-to-all-start.1) | async-done | bytes 9437216 | tf_op jit(solution)/shard_map/all_to_all | solution.py:11
  151.4 10.7 %copy.46 = bf16[3,3,8,64,4,2,128]{6,3,2,5,4,0,1:T(8,128)(2,1)} copy(bf16[3,3,8,64,4,2,128]{6,3,5,4,0,1,2:T(8,128)(2,1)} %bitcast.17) | data formatting | bytes 18874368 | tf_op jit(solution)/shard_map/reshape | solution.py:12
  162.1 0.0 copy-start.2
  162.1 0.0 copy-start.3
  162.1 8.4 %fusion.3 = f32[32,2,8,512]{3,2,1,0:T(8,128)} fusion(bf16[3,3,512,4,2,128,1,1]{5,2,4,3,7,6,0,1:T(8,128)(2,1)} %bitcast.46, f32[8,3,4,2,128]{4,0,3,2,1:T(8,128)S(1)} %multiply_bitcast_fusion, f32[32,2,3,4,2,128]{5,4,3,1,0,2:T(2,128)S(1)} %bitcast.45), kind=kOutput, calls=%fused_computation.5 | convolution fusion | flops 4841275392 | bytes 11370496 | tf_op jit(solution)/shard_map/ijdcxyz,dckxyz->ijk/dot_general | solution.py:65
  170.5 10.4 %all-to-all-start.2 = ((f32[32,2,8,512]{3,2,1,0:T(8,128)}), f32[32,2,8,512]{3,2,1,0:T(8,128)S(1)}, u32[]{:S(2)}, u32[]{:S(2)}) async-start(f32[32,2,8,512]{3,2,1,0:T(8,128)} %fusion.3), calls=%async_computation.2 | async-start | bytes 2097152 | tf_op jit(solution)/shard_map/all_to_all | solution.py:27
  180.9 0.0 copy-done.2
  180.9 0.0 copy-done.3
  181.0 29.8 %all-to-all-done.2 = f32[32,2,8,512]{3,2,1,0:T(8,128)S(1)} async-done(((f32[32,2,8,512]{3,2,1,0:T(8,128)}), f32[32,2,8,512]{3,2,1,0:T(8,128)S(1)}, u32[]{:S(2)}, u32[]{:S(2)}) %all-to-all-start.2) | async-done | bytes 1048608 | tf_op jit(solution)/shard_map/all_to_all | solution.py:27
  210.7 0.1 reduce_sum.29
  210.8 0.0 copy-start.1
  210.8 0.6 copy.47
  211.5 5.5 %gather_fusion = f32[2048,2]{1,0:T(8,128)S(1)} fusion(f32[2,4096]{0,1:T(8,128)S(1)} %bitcast.47, s32[2048]{0:T(1024)S(1)} %broadcast_clamp_fusion), kind=kCustom, calls=%fused_computation | custom fusion | bytes 40960 | tf_op jit(solution)/shard_map/jit(_take)/gather | solution.py:104
  216.9 7.1 %fusion.5 = f32[2,1024]{1,0:T(2,128)} fusion(f32[2048,1024]{1,0:T(8,128)} %param.13, f32[2048,2]{1,0:T(8,128)S(1)} %gather_fusion, pred[2048]{0:T(1024)(128)(4,1)S(1)} %compare_and_fusion), kind=kOutput, calls=%fused_computation.9 | convolution fusion | flops 50335744 | bytes 8415232 | tf_op jit(solution)/shard_map/dot_general | solution.py:105
  224.1 0.0 copy-done.1
  (5 shorter events, 0.0 us)
Async XLA Ops:
  0.6 21.4 %copy-start = (bf16[3,64,4,2,128]{4,3,2,1,0:T(2,128)(2,1)S(1)}, bf16[3,64,4,2,128]{4,3,2,1,0:T(2,128)(2,1)}, u32[]{:S(2)}) copy-start(bf16[3,64,4,2,128]{4,3,2,1,0:T(2,128)(2,1)} %param.7) | copy-start | bytes 1179652
  3.4 26.4 %collective-permute-start = (bf16[3,64,4,1,128]{4,3,2,1,0:T(2,128)(2,1)}, bf16[3,64,4,1,128]{4,3,2,1,0:T(2,128)(2,1)}, u32[]{:S(2)}, u32[]{:S(2)}) collective-permute-start(bf16[3,64,4,1,128]{4,3,2,1,0:T(2,128)(2,1)} %get-tuple-element.8), channel_id=1, source_target_pairs={{8,0},{16,8},{24,16},{32,24},{40,32},{48,40},{56,48},{64,56},{72,6... | collective-permute-start | bytes 589832 | tf_op jit(solution)/shard_map/ppermute | solution.py:39
  4.7 25.2 %collective-permute-start.1 = (bf16[3,64,4,1,128]{4,3,2,1,0:T(2,128)(2,1)}, bf16[3,64,4,1,128]{4,3,2,1,0:T(2,128)(2,1)}, u32[]{:S(2)}, u32[]{:S(2)}) collective-permute-start(bf16[3,64,4,1,128]{4,3,2,1,0:T(2,128)(2,1)} %get-tuple-element.9), channel_id=1, source_target_pairs={{0,8},{8,16},{16,24},{24,32},{32,40},{40,48},{48,56},{56,64},{64,7... | collective-permute-start | bytes 589832 | tf_op jit(solution)/shard_map/ppermute | solution.py:38
  10.6 24.6 %all-to-all-start = ((bf16[8,3,8,4,2,128]{5,2,4,3,1,0:T(8,128)(2,1)}), bf16[8,3,8,4,2,128]{5,2,4,3,1,0:T(8,128)(2,1)}, u32[]{:S(2)}, u32[]{:S(2)}) async-start(bf16[8,3,8,4,2,128]{5,2,4,3,1,0:T(8,128)(2,1)} %broadcast_in_dim.33), calls=%async_computation | async-start | bytes 786432 | tf_op jit(solution)/shard_map/all_to_all | solution.py:46
  41.2 5.8 %copy-start.4 = (s32[4,2,128]{2,1,0:T(2,128)S(1)}, s32[4,2,128]{2,1,0:T(2,128)}, u32[]{:S(2)}) copy-start(s32[4,2,128]{2,1,0:T(2,128)} %param.8) | copy-start | bytes 12292
  41.3 5.8 %copy-start.5 = (f32[8]{0:T(128)S(1)}, f32[8]{0:T(128)}, u32[]{:S(2)}) copy-start(f32[8]{0:T(128)} %param.9) | copy-start | bytes 100
  41.3 110.1 %all-to-all-start.1 = ((bf16[8,3,3,64,4,2,128]{6,3,5,4,1,2,0:T(8,128)(2,1)}), bf16[8,3,3,64,4,2,128]{6,3,5,4,1,2,0:T(8,128)(2,1)}, u32[]{:S(2)}, u32[]{:S(2)}) async-start(bf16[8,3,3,64,4,2,128]{6,3,5,4,1,2,0:T(8,128)(2,1)} %stack.8), calls=%async_computation.1 | async-start | bytes 18874368 | tf_op jit(solution)/shard_map/all_to_all | solution.py:11
  162.1 18.8 %copy-start.2 = (s32[2048]{0:T(1024)S(1)}, s32[2048]{0:T(1024)}, u32[]{:S(2)}) copy-start(s32[2048]{0:T(1024)} %param.12) | copy-start | bytes 24580
  162.1 18.8 %copy-start.3 = (s32[2048]{0:T(1024)S(1)}, s32[2048]{0:T(1024)}, u32[]{:S(2)}) copy-start(s32[2048]{0:T(1024)} %param.11) | copy-start | bytes 24580
  170.5 40.2 %all-to-all-start.2 = ((f32[32,2,8,512]{3,2,1,0:T(8,128)}), f32[32,2,8,512]{3,2,1,0:T(8,128)S(1)}, u32[]{:S(2)}, u32[]{:S(2)}) async-start(f32[32,2,8,512]{3,2,1,0:T(8,128)} %fusion.3), calls=%async_computation.2 | async-start | bytes 2097152 | tf_op jit(solution)/shard_map/all_to_all | solution.py:27
  210.8 13.3 %copy-start.1 = (f32[2,8,512]{2,1,0:T(8,128)}, f32[2,8,512]{2,1,0:T(8,128)S(1)}, u32[]{:S(2)}) copy-start(f32[2,8,512]{2,1,0:T(8,128)S(1)} %broadcast_multiply_fusion) | copy-start | bytes 98308
